TPU v7x, 32 devices: a whole 2x2x4 slice. The times are simulated.
32 devices in a mesh: dev: 8 (over z, x), ma: 4 (over y, core).
Axes of the slice: x: 2, y: 2, z: 4, core: 2. Of those that a mesh axis runs over, the one named last changes fastest.
Arguments:
- inputs: bfloat16 [8192, 2048], P('ma', 'dev'), may hold values from -6 to 6
- cotangent: bfloat16 [8192, 2048], P('ma', 'dev'), may hold values from -6 to 6
- factors: bfloat16 [4, 64, 16384], P(None, 'ma', 'dev'), may hold values from -0.5 to 0.5
- exponents: int32 [4, 64], P(None, 'ma'), may hold values from -6 to -4
- error_buffer: bfloat16 [8, 4, 64, 16384], P('dev', None, 'ma'), may hold values from -96 to 96
Outputs:
- output: bfloat16 [8192, 2048], P('ma', 'dev')
- input_grad: bfloat16 [8192, 2048], P('ma', 'dev')
- grad_mean: float32 [4, 64, 16384], P(None, 'ma', 'dev')
- new_error: bfloat16 [8, 4, 64, 16384], P('dev', None, 'ma')
All inputs are finite; a program needn't handle non-finite values.
Results may differ from a plain program's by a relative error of at most 0.0057.
Values may be sent and summed in bfloat16 or wider, within the bound.
A program may use at most 64 MiB of HBM per device.

v0:
```python
import jax
import jax.numpy as jnp
from jax import lax
from jax.sharding import PartitionSpec as P

B = 128
code_limit = 127.0


def regroup(stacked):
    groups = lax.axis_size("ma")
    count, local_blocks, width, tok_count = stacked.shape
    folded = stacked.reshape(
        count, local_blocks, width // (groups * local_blocks), groups, local_blocks, tok_count
    )
    shaped = jnp.transpose(folded, (0, 4, 2, 3, 1, 5))
    arrived = lax.all_to_all(shaped, "ma", split_axis=3, concat_axis=3, tiled=True)
    return arrived.reshape(count, local_blocks, width, tok_count)


def block_forward(weights, values):
    return jnp.einsum("ncd,nct->ndt", weights, values, preferred_element_type=jnp.float32)


def block_backward(weights, values):
    return jnp.einsum("ncd,ndt->nct", weights, values, preferred_element_type=jnp.float32)


def outer_sum(left, right):
    return jnp.einsum("nct,ndt->ncd", left, right, preferred_element_type=jnp.float32)


def quantize(gradients, error_part, exponent_part):
    totals = gradients.reshape(gradients.shape[:-2] + (-1,)) + error_part.astype(jnp.float32)
    scale_inverse = jnp.left_shift(jnp.ones_like(exponent_part), -exponent_part).astype(
        jnp.float32
    )[..., None]
    code_values = jnp.clip(totals * scale_inverse, -code_limit, code_limit)
    return (code_values, (totals - code_values / scale_inverse).astype(jnp.bfloat16), scale_inverse)


def body(inputs, cotangent, factors, exponents, error_buffer):
    local_blocks = factors.shape[1]
    tok_count = inputs.shape[1]
    group_count = lax.axis_size("dev")
    gathered = lax.all_gather(factors, "dev", axis=2, tiled=True)
    matrices = gathered.reshape(gathered.shape[0], local_blocks, B, B)
    block_in = inputs.reshape(local_blocks, B, tok_count)
    block_cot = cotangent.reshape(local_blocks, B, tok_count)
    first_out = block_forward(matrices[0], block_in).astype(jnp.bfloat16)
    mixed_one = regroup(first_out[None])[0]
    second_out = block_forward(matrices[1], mixed_one).astype(jnp.bfloat16)
    pre_gelu = regroup(second_out[None])[0]
    hidden_wide, gelu_back = jax.vjp(jax.nn.gelu, pre_gelu.astype(jnp.float32))
    hidden = hidden_wide.astype(jnp.bfloat16)
    third_out = block_forward(matrices[2], hidden).astype(jnp.bfloat16)
    mixed_two = regroup(third_out[None])[0]
    fourth_out = block_forward(matrices[3], mixed_two).astype(jnp.bfloat16)
    returned = regroup(fourth_out[None])[0]
    output = (block_in.astype(jnp.float32) + returned.astype(jnp.float32)).astype(jnp.bfloat16)
    back_four = regroup(block_cot[None])[0]
    d_mixed_two = block_backward(matrices[3], back_four).astype(jnp.bfloat16)
    gradient_three = outer_sum(mixed_two, back_four)
    d_third = regroup(d_mixed_two[None])[0]
    d_pre = gelu_back(block_backward(matrices[2], d_third))[0].astype(jnp.bfloat16)
    gradient_two = outer_sum(hidden, d_third)
    d_second = regroup(d_pre[None])[0]
    d_mixed_one = block_backward(matrices[1], d_second).astype(jnp.bfloat16)
    gradient_one = outer_sum(mixed_one, d_second)
    d_first = regroup(d_mixed_one[None])[0]
    input_grad = (block_cot.astype(jnp.float32) + block_backward(matrices[0], d_first)).astype(
        jnp.bfloat16
    )
    gradient_zero = outer_sum(block_in, d_first)
    gradients = jnp.stack([gradient_zero, gradient_one, gradient_two, gradient_three])
    code_values, new_part, scale_inverse = quantize(gradients, error_buffer[0], exponents)
    summed = lax.psum_scatter(code_values, "dev", scatter_dimension=2, tiled=True)
    grad_mean = summed / scale_inverse / group_count
    new_error = new_part[None]
    return (
        output.reshape(local_blocks * B, tok_count),
        input_grad.reshape(local_blocks * B, tok_count),
        grad_mean,
        new_error,
    )


def solution(mesh):
    in_specs = (
        P("ma", "dev"),
        P("ma", "dev"),
        P(None, "ma", "dev"),
        P(None, "ma"),
        P("dev", None, "ma", None),
    )
    out_specs = (P("ma", "dev"), P("ma", "dev"), P(None, "ma", "dev"), P("dev", None, "ma", None))
    return jax.shard_map(body, mesh=mesh, in_specs=in_specs, out_specs=out_specs, check_vma=False)
```

profile of v0, /device:TPU:0, one launch (start us, length us, event | category | flops | bytes accessed | tf_op | source)
XLA Modules:
  0.0 293.5 jit_solution(14815720484470332092)
XLA Ops:
  7.2 0.7 all-gather.2.cloned.1.call-update
  7.9 2.8 copy.67
  10.7 4.3 %all-to-all-start.4 = ((bf16[1,16,2,4,16,256]{5,4,2,1,0,3:T(8,128)(2,1)}), bf16[1,16,2,4,16,256]{5,4,2,1,0,3:T(8,128)(2,1)S(1)}, u32[]{:S(2)}, u32[]{:S(2)}) async-start(bf16[1,16,2,4,16,256]{5,4,2,1,0,3:T(8,128)(2,1)} %copy.67), calls=%async_computation.4 | async-start | bytes 2097152 | tf_op jit(solution)/shard_map/all_to_all | solution.py:17
  14.9 47.0 %all-gather.2.cloned.1.call-done = bf16[4,16,16384]{2,1,0:T(8,128)(2,1)} async-done(((bf16[4,16,2048]{2,1,0:T(8,128)(2,1)}), bf16[4,16,16384]{2,1,0:T(8,128)(2,1)}) %all-gather.2.cloned.1.call-update) | async-done | bytes 2097168 | tf_op jit(solution)/shard_map/all_gather | solution.py:46
  62.0 2.7 slice_bitcast_fusion
  64.8 0.8 copy-done.9
  65.6 0.5 convolution_convert_fusion.5
  66.1 1.1 copy.98
  67.2 4.2 %all-to-all-start = ((bf16[1,16,2,4,16,256]{5,1,2,4,0,3:T(8,128)(2,1)}), bf16[1,16,2,4,16,256]{5,1,2,4,0,3:T(8,128)(2,1)}, u32[]{:S(2)}, u32[]{:S(2)}) async-start(bf16[1,16,2,4,16,256]{5,1,2,4,0,3:T(8,128)(2,1)} %bitcast.115), calls=%async_computation | async-start | bytes 2097152 | tf_op jit(solution)/shard_map/all_to_all | solution.py:17
  71.6 0.9 copy-done.21
  72.6 0.8 copy-done.11
  73.8 1.1 copy.94
  74.9 11.0 %all-to-all-done = bf16[1,16,2,4,16,256]{5,1,2,4,0,3:T(8,128)(2,1)} async-done(((bf16[1,16,2,4,16,256]{5,1,2,4,0,3:T(8,128)(2,1)}), bf16[1,16,2,4,16,256]{5,1,2,4,0,3:T(8,128)(2,1)}, u32[]{:S(2)}, u32[]{:S(2)}) %all-to-all-start) | async-done | bytes 1048608 | tf_op jit(solution)/shard_map/all_to_all | solution.py:17
  85.9 4.2 %all-to-all-start.5 = ((bf16[1,16,2,4,16,256]{5,1,2,4,0,3:T(8,128)(2,1)}), bf16[1,16,2,4,16,256]{5,1,2,4,0,3:T(8,128)(2,1)}, u32[]{:S(2)}, u32[]{:S(2)}) async-start(bf16[1,16,2,4,16,256]{5,1,2,4,0,3:T(8,128)(2,1)} %bitcast.111), calls=%async_computation.5 | async-start | bytes 2097152 | tf_op jit(solution)/shard_map/all_to_all | solution.py:17
  90.3 2.0 copy.57
  92.3 0.5 convolution_convert_fusion.4
  92.8 1.1 copy.97
  93.9 10.8 %all-to-all-done.5 = bf16[1,16,2,4,16,256]{5,1,2,4,0,3:T(8,128)(2,1)} async-done(((bf16[1,16,2,4,16,256]{5,1,2,4,0,3:T(8,128)(2,1)}), bf16[1,16,2,4,16,256]{5,1,2,4,0,3:T(8,128)(2,1)}, u32[]{:S(2)}, u32[]{:S(2)}) %all-to-all-start.5) | async-done | bytes 1048608 | tf_op jit(solution)/shard_map/all_to_all | solution.py:17
  104.7 4.2 %all-to-all-start.1 = ((bf16[1,16,2,4,16,256]{5,1,2,4,0,3:T(8,128)(2,1)}), bf16[1,16,2,4,16,256]{5,1,2,4,0,3:T(8,128)(2,1)}, u32[]{:S(2)}, u32[]{:S(2)}) async-start(bf16[1,16,2,4,16,256]{5,1,2,4,0,3:T(8,128)(2,1)} %bitcast.138), calls=%async_computation.1 | async-start | bytes 2097152 | tf_op jit(solution)/shard_map/all_to_all | solution.py:17
  108.9 1.9 copy.83
  110.9 2.8 copy.70
  113.6 9.8 %all-to-all-done.1 = bf16[1,16,2,4,16,256]{5,1,2,4,0,3:T(8,128)(2,1)} async-done(((bf16[1,16,2,4,16,256]{5,1,2,4,0,3:T(8,128)(2,1)}), bf16[1,16,2,4,16,256]{5,1,2,4,0,3:T(8,128)(2,1)}, u32[]{:S(2)}, u32[]{:S(2)}) %all-to-all-start.1) | async-done | bytes 1048608 | tf_op jit(solution)/shard_map/all_to_all | solution.py:17
  123.4 2.0 copy.60
  125.4 1.6 fusion.9
  127.0 1.1 copy.93
  128.1 4.2 %all-to-all-start.6 = ((bf16[1,16,2,4,16,256]{5,1,2,4,0,3:T(8,128)(2,1)}), bf16[1,16,2,4,16,256]{5,1,2,4,0,3:T(8,128)(2,1)}, u32[]{:S(2)}, u32[]{:S(2)}) async-start(bf16[1,16,2,4,16,256]{5,1,2,4,0,3:T(8,128)(2,1)} %bitcast.140), calls=%async_computation.6 | async-start | bytes 2097152 | tf_op jit(solution)/shard_map/all_to_all | solution.py:17
  132.4 2.6 convolution_convert_fusion.3
  135.0 1.1 copy.96
  136.1 10.8 %all-to-all-done.6 = bf16[1,16,2,4,16,256]{5,1,2,4,0,3:T(8,128)(2,1)} async-done(((bf16[1,16,2,4,16,256]{5,1,2,4,0,3:T(8,128)(2,1)}), bf16[1,16,2,4,16,256]{5,1,2,4,0,3:T(8,128)(2,1)}, u32[]{:S(2)}, u32[]{:S(2)}) %all-to-all-start.6) | async-done | bytes 1048608 | tf_op jit(solution)/shard_map/all_to_all | solution.py:17
  146.8 4.2 %all-to-all-start.2 = ((bf16[1,16,2,4,16,256]{5,1,2,4,0,3:T(8,128)(2,1)}), bf16[1,16,2,4,16,256]{5,1,2,4,0,3:T(8,128)(2,1)}, u32[]{:S(2)}, u32[]{:S(2)}) async-start(bf16[1,16,2,4,16,256]{5,1,2,4,0,3:T(8,128)(2,1)} %bitcast.137), calls=%async_computation.2 | async-start | bytes 2097152 | tf_op jit(solution)/shard_map/all_to_all | solution.py:17
  151.1 1.9 copy.72
  153.0 1.0 copy-done.5
  154.4 1.1 copy.92
  155.6 10.0 %all-to-all-done.2 = bf16[1,16,2,4,16,256]{5,1,2,4,0,3:T(8,128)(2,1)} async-done(((bf16[1,16,2,4,16,256]{5,1,2,4,0,3:T(8,128)(2,1)}), bf16[1,16,2,4,16,256]{5,1,2,4,0,3:T(8,128)(2,1)}, u32[]{:S(2)}, u32[]{:S(2)}) %all-to-all-start.2) | async-done | bytes 1048608 | tf_op jit(solution)/shard_map/all_to_all | solution.py:17
  165.6 4.2 %all-to-all-start.7 = ((bf16[1,16,2,4,16,256]{5,1,2,4,0,3:T(8,128)(2,1)}), bf16[1,16,2,4,16,256]{5,1,2,4,0,3:T(8,128)(2,1)}, u32[]{:S(2)}, u32[]{:S(2)}) async-start(bf16[1,16,2,4,16,256]{5,1,2,4,0,3:T(8,128)(2,1)} %bitcast.136), calls=%async_computation.7 | async-start | bytes 2097152 | tf_op jit(solution)/shard_map/all_to_all | solution.py:17
  170.1 3.6 %fusion.15 = f32[16,128,128]{2,1,0:T(8,128)} fusion(bf16[16,128,256]{2,1,0:T(8,128)(2,1)} %bitcast.150, f32[16,128,256]{2,1,0:T(8,128)} %bitcast.148), kind=kOutput, calls=%fused_computation.45 | convolution fusion | flops 138936320 | bytes 4194304 | tf_op jit(solution)/shard_map/nct,ndt->ncd/dot_general | solution.py:30
  173.7 2.4 stack.27
  176.1 2.6 fusion.16
  178.8 2.4 stack.26
  181.2 1.8 copy.63
  183.0 1.0 copy-done.3
  183.9 0.4 fusion.17
  184.4 1.3 stack.28
  185.7 1.8 copy.74
  187.5 1.5 convolution_bitcast_fusion
  189.0 1.6 copy.75
  190.6 1.4 stack.25
  192.0 5.4 %fusion.2 = f32[4,16,16384]{2,1,0:T(8,128)} fusion(bf16[1,4,16,16384]{3,2,1,0:T(8,128)(2,1)} %param.9, f32[1,16,16384]{2,1,0:T(8,128)} %stack.28, f32[1,16,16384]{2,1,0:T(8,128)} %stack.27, f32[1,16,16384]{2,1,0:T(8,128)} %stack.26, f32[1,16,16384]{2,1,0:T(8,128)} %stack.25, f32[4,16]{1,0:T(4,128)S(1)} %shift-left_convert_fusion), kind=kLoop, calls=%fused_computation.4 | loop fusion | flops 7340032 | bytes 10486016 | tf_op jit(solution)/shard_map/jit(clip)/min | solution.py:38
  197.4 1.2 copy-done.4
  198.6 1.5 convolution_convert_fusion.2
  200.1 1.1 copy.95
  201.2 4.4 %all-to-all-start.3 = ((bf16[1,16,2,4,16,256]{5,1,2,4,0,3:T(8,128)(2,1)}), bf16[1,16,2,4,16,256]{5,1,2,4,0,3:T(8,128)(2,1)}, u32[]{:S(2)}, u32[]{:S(2)}) async-start(bf16[1,16,2,4,16,256]{5,1,2,4,0,3:T(8,128)(2,1)} %bitcast.139), calls=%async_computation.3 | async-start | bytes 2097152 | tf_op jit(solution)/shard_map/all_to_all | solution.py:17
  205.6 2.4 stack.32
  208.0 1.2 stack.31
  209.2 2.5 stack.33
  211.7 1.2 stack.30
  212.8 7.2 %all-to-all-done.3 = bf16[1,16,2,4,16,256]{5,1,2,4,0,3:T(8,128)(2,1)} async-done(((bf16[1,16,2,4,16,256]{5,1,2,4,0,3:T(8,128)(2,1)}), bf16[1,16,2,4,16,256]{5,1,2,4,0,3:T(8,128)(2,1)}, u32[]{:S(2)}, u32[]{:S(2)}) %all-to-all-start.3) | async-done | bytes 1048608 | tf_op jit(solution)/shard_map/all_to_all | solution.py:17
  220.1 1.9 copy.66
  222.1 1.4 fusion.10
  223.5 1.3 fusion.11
  224.8 0.9 copy-done.8
  225.9 1.9 subtract_convert_fusion
  227.9 56.8 %reduce-scatter.2.cloned.1.call-done = f32[4,16,2048]{2,1,0:T(8,128)} async-done(((f32[4,16,16384]{2,1,0:T(8,128)}), f32[4,16,2048]{2,1,0:T(8,128)}) %reduce-scatter.2.cloned.1.call-update) | async-done | bytes 524304 | tf_op jit(solution)/shard_map/reduce_scatter | solution.py:77
  284.7 1.9 divide_multiply_fusion
  (55 shorter events, 1.9 us)
Async XLA Ops:
  7.2 54.8 %all-gather.2.cloned.1.call-start = ((), (), s32[]{:S(2)}) async-start(), calls=%async_computation.9 | async-start | bytes 2359296 | tf_op jit(solution)/shard_map/all_gather | solution.py:46
  10.7 56.5 %all-to-all-start.4 = ((bf16[1,16,2,4,16,256]{5,4,2,1,0,3:T(8,128)(2,1)}), bf16[1,16,2,4,16,256]{5,4,2,1,0,3:T(8,128)(2,1)S(1)}, u32[]{:S(2)}, u32[]{:S(2)}) async-start(bf16[1,16,2,4,16,256]{5,4,2,1,0,3:T(8,128)(2,1)} %copy.67), calls=%async_computation.4 | async-start | bytes 2097152 | tf_op jit(solution)/shard_map/all_to_all | solution.py:17
  14.9 50.6 %copy-start = (bf16[2048,256]{1,0:T(8,128)(2,1)S(1)}, bf16[2048,256]{1,0:T(8,128)(2,1)}, u32[]{:S(2)}) copy-start(bf16[2048,256]{1,0:T(8,128)(2,1)} %param.5) | copy-start | bytes 3145732
  64.8 0.8 copy-start.9
  67.2 18.7 %all-to-all-start = ((bf16[1,16,2,4,16,256]{5,1,2,4,0,3:T(8,128)(2,1)}), bf16[1,16,2,4,16,256]{5,1,2,4,0,3:T(8,128)(2,1)}, u32[]{:S(2)}, u32[]{:S(2)}) async-start(bf16[1,16,2,4,16,256]{5,1,2,4,0,3:T(8,128)(2,1)} %bitcast.115), calls=%async_computation | async-start | bytes 2097152 | tf_op jit(solution)/shard_map/all_to_all | solution.py:17
  71.4 1.0 copy-start.21
  72.6 0.8 copy-start.11
  73.8 16.4 %copy-start.20 = (bf16[2,8,128,128]{3,1,2,0:T(8,128)(2,1)S(1)}, bf16[2,8,128,128]{3,1,2,0:T(8,128)(2,1)}, u32[]{:S(2)}) copy-start(bf16[2,8,128,128]{3,1,2,0:T(8,128)(2,1)} %get-tuple-element.6) | copy-start | bytes 1572868
  85.9 18.7 %all-to-all-start.5 = ((bf16[1,16,2,4,16,256]{5,1,2,4,0,3:T(8,128)(2,1)}), bf16[1,16,2,4,16,256]{5,1,2,4,0,3:T(8,128)(2,1)}, u32[]{:S(2)}, u32[]{:S(2)}) async-start(bf16[1,16,2,4,16,256]{5,1,2,4,0,3:T(8,128)(2,1)} %bitcast.111), calls=%async_computation.5 | async-start | bytes 2097152 | tf_op jit(solution)/shard_map/all_to_all | solution.py:17
  90.3 2.5 copy-start.12
  104.7 18.7 %all-to-all-start.1 = ((bf16[1,16,2,4,16,256]{5,1,2,4,0,3:T(8,128)(2,1)}), bf16[1,16,2,4,16,256]{5,1,2,4,0,3:T(8,128)(2,1)}, u32[]{:S(2)}, u32[]{:S(2)}) async-start(bf16[1,16,2,4,16,256]{5,1,2,4,0,3:T(8,128)(2,1)} %bitcast.138), calls=%async_computation.1 | async-start | bytes 2097152 | tf_op jit(solution)/shard_map/all_to_all | solution.py:17
  123.4 2.0 copy-start.22
  123.4 2.0 copy-start.23
  125.4 1.6 copy-start.19
  128.1 18.7 %all-to-all-start.6 = ((bf16[1,16,2,4,16,256]{5,1,2,4,0,3:T(8,128)(2,1)}), bf16[1,16,2,4,16,256]{5,1,2,4,0,3:T(8,128)(2,1)}, u32[]{:S(2)}, u32[]{:S(2)}) async-start(bf16[1,16,2,4,16,256]{5,1,2,4,0,3:T(8,128)(2,1)} %bitcast.140), calls=%async_computation.6 | async-start | bytes 2097152 | tf_op jit(solution)/shard_map/all_to_all | solution.py:17
  135.0 16.2 %copy-start.24 = (s32[4,16]{1,0:T(4,128)S(1)}, s32[4,16]{1,0:T(4,128)}, u32[]{:S(2)}) copy-start(s32[4,16]{1,0:T(4,128)} %param.8) | copy-start | bytes 772
  146.8 18.7 %all-to-all-start.2 = ((bf16[1,16,2,4,16,256]{5,1,2,4,0,3:T(8,128)(2,1)}), bf16[1,16,2,4,16,256]{5,1,2,4,0,3:T(8,128)(2,1)}, u32[]{:S(2)}, u32[]{:S(2)}) async-start(bf16[1,16,2,4,16,256]{5,1,2,4,0,3:T(8,128)(2,1)} %bitcast.137), calls=%async_computation.2 | async-start | bytes 2097152 | tf_op jit(solution)/shard_map/all_to_all | solution.py:17
  151.1 2.9 copy-start.13
  153.0 1.0 copy-start.5
  165.6 20.1 %all-to-all-start.7 = ((bf16[1,16,2,4,16,256]{5,1,2,4,0,3:T(8,128)(2,1)}), bf16[1,16,2,4,16,256]{5,1,2,4,0,3:T(8,128)(2,1)}, u32[]{:S(2)}, u32[]{:S(2)}) async-start(bf16[1,16,2,4,16,256]{5,1,2,4,0,3:T(8,128)(2,1)} %bitcast.136), calls=%async_computation.7 | async-start | bytes 2097152 | tf_op jit(solution)/shard_map/all_to_all | solution.py:17
  169.9 114.8 %reduce-scatter.2.cloned.1.call-start = ((), (), s32[]{:S(2)}) async-start(), calls=%async_computation.10 | async-start | bytes 4718592 | tf_op jit(solution)/shard_map/reduce_scatter | solution.py:77
  183.0 1.0 copy-start.3
  184.4 3.1 %copy-start.2 = (f32[16,128,128]{2,1,0:T(8,128)}, f32[16,128,128]{2,1,0:T(8,128)S(1)}, u32[]{:S(2)}) copy-start(f32[16,128,128]{2,1,0:T(8,128)S(1)} %fusion.17) | copy-start | bytes 3145732
  190.6 6.8 %copy-start.6 = (f32[16,128,128]{2,1,0:T(8,128)}, f32[16,128,128]{2,1,0:T(8,128)S(1)}, u32[]{:S(2)}) copy-start(f32[16,128,128]{2,1,0:T(8,128)S(1)} %copy.75) | copy-start | bytes 3145732
  197.3 1.2 copy-start.4
  201.2 6.8 %copy-start.1 = (f32[16,128,128]{2,1,0:T(8,128)S(1)}, f32[16,128,128]{2,1,0:T(8,128)}, u32[]{:S(2)}) copy-start(f32[16,128,128]{2,1,0:T(8,128)} %fusion.16) | copy-start | bytes 3145732
  201.2 18.9 %all-to-all-start.3 = ((bf16[1,16,2,4,16,256]{5,1,2,4,0,3:T(8,128)(2,1)}), bf16[1,16,2,4,16,256]{5,1,2,4,0,3:T(8,128)(2,1)}, u32[]{:S(2)}, u32[]{:S(2)}) async-start(bf16[1,16,2,4,16,256]{5,1,2,4,0,3:T(8,128)(2,1)} %bitcast.139), calls=%async_computation.3 | async-start | bytes 2097152 | tf_op jit(solution)/shard_map/all_to_all | solution.py:17
  209.2 2.5 copy-start.7
  212.8 9.2 %copy-start.10 = (bf16[2,8,128,128]{3,2,1,0:T(8,128)(2,1)S(1)}, bf16[2,8,128,128]{3,2,1,0:T(8,128)(2,1)}, u32[]{:S(2)}) copy-start(bf16[2,8,128,128]{3,2,1,0:T(8,128)(2,1)} %copy-done.9) | copy-start | bytes 1572868
  220.1 1.9 copy-start.14
  222.0 2.7 copy-start.16
  222.0 2.7 copy-start.17
  222.0 2.7 copy-start.18
  223.5 2.2 copy-start.8
  223.5 2.5 copy-start.15
Sparse Core Ops, SparseCore 0:
  10.2 51.7 all-gather.1
  197.5 87.1 reduce-scatter.1
where the time goes:
time: 295 us; the launch traced here: 293 us
  waiting for transfers between devices  164 us (56%)
  local copies, waits for them, and re-layouts  52.9 us (18%)
  starting transfers between devices  34.4 us (12%)
  matrix products  17.1 us (6%)
  between operations  14.4 us (5%)
  other arithmetic  10.6 us (4%)
    all_to_all x8, waiting for transfers between devices, regroup(): lax.all_to_all(shaped, 'ma', split_axis=3, concat_axis=3, tiled=True)  59.6 us
    reduce_scatter x1, waiting for transfers between devices, body(): lax.psum_scatter(code_values, 'dev', scatter_dimension=2, tiled=True)  56.8 us
    all_gather x1, waiting for transfers between devices, body(): gathered = lax.all_gather(factors, 'dev', axis=2, tiled=True)  47 us
    all_to_all x8, starting transfers between devices, regroup(): lax.all_to_all(shaped, 'ma', split_axis=3, concat_axis=3, tiled=True)  34.1 us
    another operation x8, local copies, waits for them, and re-layouts, body(): jnp.stack([gradient_zero, gradient_one, gradient_two, gradient_three])  14.7 us
    all_to_all x7, local copies, waits for them, and re-layouts, regroup(): lax.all_to_all(shaped, 'ma', split_axis=3, concat_axis=3, tiled=True)  12.3 us
    unnamed x55, local copies, waits for them, and re-layouts  11.8 us
    dot_general x4, matrix products, outer_sum(): jnp.einsum('nct,ndt->ncd', left, right, preferred_element_type=jnp.float32)  8.22 us
  transfers between devices with their start and end apart: 10, of which 8 were waited for; matrix products, arithmetic and copies ran while one was open for 19% of the time, Pallas kernels for 0%

commit v1 on v0

--- a/solution.py
+++ b/solution.py
@@ -7,14 +7,41 @@
 code_limit = 127.0
 
 
+def tiles_resolve(matrix, at_axis, array_in):
+    parts_out = matrix.shape
+    b_now = matrix.reshape(
+        *parts_out[:at_axis], array_in, parts_out[at_axis] // array_in, *parts_out[at_axis + 1 :]
+    )
+    return jnp.moveaxis(b_now, at_axis, 0)
+
+
+def show_ladders(xin, which_dim):
+    known = list(xin.shape[1:])
+    known[which_dim] *= xin.shape[0]
+    return jnp.moveaxis(xin, 0, which_dim).reshape(known)
+
+
 def regroup(stacked):
+
+    def refer_ratios(row_axis, panel, original, target):
+        p_next, v1 = (lax.axis_size(row_axis), lax.axis_index(row_axis))
+        state_next = tiles_resolve(original, target, p_next)
+        panels = [state_next[v1]]
+        for rr in range(1, p_next):
+            local_now = state_next[v1 ^ rr]
+            panels.append(
+                lax.ppermute(local_now, row_axis, [(jj, jj ^ rr) for jj in range(p_next)])
+            )
+        state_next = jnp.stack(panels, 0)[v1 ^ jnp.arange(p_next)]
+        return show_ladders(state_next, panel)
+
     groups = lax.axis_size("ma")
     count, local_blocks, width, tok_count = stacked.shape
     folded = stacked.reshape(
         count, local_blocks, width // (groups * local_blocks), groups, local_blocks, tok_count
     )
     shaped = jnp.transpose(folded, (0, 4, 2, 3, 1, 5))
-    arrived = lax.all_to_all(shaped, "ma", split_axis=3, concat_axis=3, tiled=True)
+    arrived = refer_ratios("ma", 3, shaped, 3)
     return arrived.reshape(count, local_blocks, width, tok_count)
 
 

time: 295 us -> 274 us (0.929)
  starting transfers between devices: 34.4 us -> 18.3 us
  waiting for transfers between devices: 164 us -> 152 us
  other arithmetic: 10.6 us -> 20.8 us
  matrix products: 17.1 us -> 11.8 us
    all_to_all x8 -> x0, waiting for transfers between devices: 59.6 us -> none  [regroup(): lax.all_to_all(shaped, 'ma', split_axis=3, concat_axis=3, tiled=True)]
    ppermute x0 -> x24, waiting for transfers between devices: none -> 55.8 us  [refer_ratios(): lax.ppermute(local_now, row_axis, [(jj, jj ^ rr) for jj in range(p_next)])]
    all_to_all x8 -> x0, starting transfers between devices: 34.1 us -> none  [regroup(): lax.all_to_all(shaped, 'ma', split_axis=3, concat_axis=3, tiled=True)]
    ppermute x0 -> x24, starting transfers between devices: none -> 18.3 us  [refer_ratios(): lax.ppermute(local_now, row_axis, [(jj, jj ^ rr) for jj in range(p_next)])]
    all_to_all x7 -> x0, local copies, waits for them, and re-layouts: 12.3 us -> none  [regroup(): lax.all_to_all(shaped, 'ma', split_axis=3, concat_axis=3, tiled=True)]
    gather x0 -> x8, local copies, waits for them, and re-layouts: none -> 12.2 us  [refer_ratios(): state_next = jnp.stack(panels, 0)[v1 ^ jnp.arange(p_next)]]
    all_gather x1, waiting for transfers between devices: 47 us -> 35.7 us  [body(): gathered = lax.all_gather(factors, 'dev', axis=2, tiled=True)]
    another operation x0 -> x8, other arithmetic: none -> 9.72 us  [refer_ratios(): state_next = jnp.stack(panels, 0)[v1 ^ jnp.arange(p_next)]]
  transfers between devices with their start and end apart: 10 -> 26, of which waited for: 8 -> 13; matrix products, arithmetic and copies ran while one was open for 19% -> 17% of each run, Pallas kernels for 0% -> 0%
where the time goes in v1:
time: 274 us; the launch traced here: 273 us
  waiting for transfers between devices  152 us (55%)
  local copies, waits for them, and re-layouts  55.4 us (20%)
  other arithmetic  20.8 us (8%)
  starting transfers between devices  18.3 us (7%)
  between operations  14.5 us (5%)
  matrix products  11.8 us (4%)
    reduce_scatter x1, waiting for transfers between devices, body(): lax.psum_scatter(code_values, 'dev', scatter_dimension=2, tiled=True)  60 us
    ppermute x24, waiting for transfers between devices, refer_ratios(): lax.ppermute(local_now, row_axis, [(jj, jj ^ rr) for jj in range(p_next)])  55.8 us
    all_gather x1, waiting for transfers between devices, body(): gathered = lax.all_gather(factors, 'dev', axis=2, tiled=True)  35.7 us
    ppermute x24, starting transfers between devices, refer_ratios(): lax.ppermute(local_now, row_axis, [(jj, jj ^ rr) for jj in range(p_next)])  18.3 us
    another operation x8, local copies, waits for them, and re-layouts, body(): jnp.stack([gradient_zero, gradient_one, gradient_two, gradient_three])  12.3 us
    gather x8, local copies, waits for them, and re-layouts, refer_ratios(): state_next = jnp.stack(panels, 0)[v1 ^ jnp.arange(p_next)]  12.2 us
    transpose x6, local copies, waits for them, and re-layouts, show_ladders(): return jnp.moveaxis(xin, 0, which_dim).reshape(known)  11.8 us
    another operation x8, other arithmetic, refer_ratios(): state_next = jnp.stack(panels, 0)[v1 ^ jnp.arange(p_next)]  9.72 us
  transfers between devices with their start and end apart: 26, of which 13 were waited for; matrix products, arithmetic and copies ran while one was open for 17% of the time, Pallas kernels for 0%

profile of v1, /device:TPU:0, one launch (start us, length us, event | category | flops | bytes accessed | tf_op | source)
XLA Modules:
  0.0 273.0 jit_solution(2564828168525342323)
XLA Ops:
  8.0 1.3 dynamic-slice_bitcast_fusion.15
  9.8 2.6 collective-permute-start.14
  12.5 6.6 %collective-permute-done.14 = bf16[1,16,2,1,16,256]{5,1,3,2,4,0:T(8,128)(2,1)S(1)} collective-permute-done((bf16[1,16,2,1,16,256]{5,1,3,2,4,0:T(8,128)(2,1)S(1)}, bf16[1,16,2,1,16,256]{5,1,3,2,4,0:T(8,128)(2,1)S(1)}, u32[]{:S(2)}, u32[]{:S(2)}) %collective-permute-start.14) | collective-permute-done | bytes 262176 | tf_op jit(solution)/shard_map/ppermute | solution.py:33
  19.1 5.8 %collective-permute-done.13 = bf16[1,16,2,1,16,256]{5,1,2,4,3,0:T(8,128)(2,1)S(1)} collective-permute-done((bf16[1,16,2,1,16,256]{5,1,2,4,3,0:T(8,128)(2,1)S(1)}, bf16[1,16,2,1,16,256]{5,1,2,4,3,0:T(8,128)(2,1)S(1)}, u32[]{:S(2)}, u32[]{:S(2)}) %collective-permute-start.13) | collective-permute-done | bytes 262176 | tf_op jit(solution)/shard_map/ppermute | solution.py:33
  26.3 35.7 %all-gather.2.cloned.1.call-done = bf16[4,16,16384]{2,1,0:T(8,128)(2,1)} async-done(((bf16[4,16,2048]{2,1,0:T(8,128)(2,1)}), bf16[4,16,16384]{2,1,0:T(8,128)(2,1)}) %all-gather.2.cloned.1.call-update) | async-done | bytes 2097168 | tf_op jit(solution)/shard_map/all_gather | solution.py:73
  62.0 1.7 slice_bitcast_fusion
  63.9 1.4 copy-done
  65.9 1.6 collective-permute-start.2
  68.6 1.0 dynamic-slice_bitcast_fusion.11
  69.6 1.6 collective-permute-start.17
  71.8 2.4 collective-permute-done.2
  74.2 6.6 %collective-permute-done.1 = bf16[1,16,2,1,16,256]{5,1,2,4,3,0:T(8,128)(2,1)S(1)} collective-permute-done((bf16[1,16,2,1,16,256]{5,1,2,4,3,0:T(8,128)(2,1)S(1)}, bf16[1,16,2,1,16,256]{5,1,2,4,3,0:T(8,128)(2,1)S(1)}, u32[]{:S(2)}, u32[]{:S(2)}) %collective-permute-start.1) | collective-permute-done | bytes 262176 | tf_op jit(solution)/shard_map/ppermute | solution.py:33
  81.0 1.6 gather_fusion
  82.6 1.8 copy.49
  84.9 1.0 dynamic-slice_bitcast_fusion.27
  85.9 1.6 collective-permute-start.5
  89.0 3.2 %collective-permute-done.16 = bf16[1,16,2,1,16,256]{5,1,2,4,3,0:T(8,128)(2,1)} collective-permute-done((bf16[1,16,2,1,16,256]{5,1,2,4,3,0:T(8,128)(2,1)}, bf16[1,16,2,1,16,256]{5,1,2,4,3,0:T(8,128)(2,1)}, u32[]{:S(2)}, u32[]{:S(2)}) %collective-permute-start.16) | collective-permute-done | bytes 262176 | tf_op jit(solution)/shard_map/ppermute | solution.py:33
  92.2 1.2 maximum_bitcast_fusion.5
  93.4 1.6 gather_fusion.5
  95.0 2.8 %copy.72 = bf16[1,16,2,4,1,16,256]{6,5,3,2,1,4,0:T(8,128)(2,1)} copy(bf16[1,16,2,4,1,16,256]{6,1,2,5,3,4,0:T(8,128)(2,1)} %bitcast.321) | data formatting | bytes 2097152 | tf_op jit(solution)/shard_map/transpose | solution.py:21
  97.8 5.0 %collective-permute-done.4 = bf16[1,16,2,1,16,256]{5,1,2,4,3,0:T(8,128)(2,1)} collective-permute-done((bf16[1,16,2,1,16,256]{5,1,2,4,3,0:T(8,128)(2,1)}, bf16[1,16,2,1,16,256]{5,1,2,4,3,0:T(8,128)(2,1)}, u32[]{:S(2)}, u32[]{:S(2)}) %collective-permute-start.4) | collective-permute-done | bytes 262176 | tf_op jit(solution)/shard_map/ppermute | solution.py:33
  102.8 2.2 maximum_bitcast_fusion.1
  105.0 1.8 gather_fusion.1
  107.2 1.2 copy.54
  110.2 1.6 collective-permute-start.8
  111.8 1.6 fusion.9
  113.4 1.0 dynamic-slice_bitcast_fusion.7
  115.1 1.5 collective-permute-start.19
  117.3 1.4 stack.155
  119.2 5.2 %collective-permute-done.20 = bf16[1,16,2,1,16,256]{5,1,3,2,4,0:T(8,128)(2,1)} collective-permute-done((bf16[1,16,2,1,16,256]{5,1,3,2,4,0:T(8,128)(2,1)}, bf16[1,16,2,1,16,256]{5,1,3,2,4,0:T(8,128)(2,1)}, u32[]{:S(2)}, u32[]{:S(2)}) %collective-permute-start.20) | collective-permute-done | bytes 262176 | tf_op jit(solution)/shard_map/ppermute | solution.py:33
  124.5 6.6 %collective-permute-done.19 = bf16[1,16,2,1,16,256]{5,1,2,4,3,0:T(8,128)(2,1)} collective-permute-done((bf16[1,16,2,1,16,256]{5,1,2,4,3,0:T(8,128)(2,1)}, bf16[1,16,2,1,16,256]{5,1,2,4,3,0:T(8,128)(2,1)}, u32[]{:S(2)}, u32[]{:S(2)}) %collective-permute-start.19) | collective-permute-done | bytes 262176 | tf_op jit(solution)/shard_map/ppermute | solution.py:33
  131.1 1.3 maximum_bitcast_fusion.6
  132.4 1.6 gather_fusion.6
  134.0 2.0 copy.76
  137.5 2.2 maximum_bitcast_fusion.2
  139.7 2.8 %gather_fusion.2 = bf16[4,16,2,16,256]{4,1,2,3,0:T(8,128)(2,1)} fusion(bf16[4,16,2,16,256]{4,1,2,3,0:T(8,128)(2,1)} %maximum_bitcast_fusion.2, s32[1024]{0:T(1024)S(1)} %pad_clamp_fusion), kind=kCustom, calls=%fused_computation.2 | custom fusion | bytes 2097168 | tf_op jit(solution)/shard_map/gather | solution.py:35
  142.5 2.8 %copy.59 = bf16[1,16,2,4,1,16,256]{6,5,3,2,1,4,0:T(8,128)(2,1)} copy(bf16[1,16,2,4,1,16,256]{6,1,2,5,3,4,0:T(8,128)(2,1)} %bitcast.323) | data formatting | bytes 2097152 | tf_op jit(solution)/shard_map/transpose | solution.py:21
  146.2 1.6 collective-permute-start.23
  148.3 1.2 stack.154
  149.6 1.7 fusion.18
  151.2 1.2 stack.156
  152.4 2.4 collective-permute-done.23
  154.8 5.9 %collective-permute-done.22 = bf16[1,16,2,1,16,256]{5,1,2,4,3,0:T(8,128)(2,1)} collective-permute-done((bf16[1,16,2,1,16,256]{5,1,2,4,3,0:T(8,128)(2,1)}, bf16[1,16,2,1,16,256]{5,1,2,4,3,0:T(8,128)(2,1)}, u32[]{:S(2)}, u32[]{:S(2)}) %collective-permute-start.22) | collective-permute-done | bytes 262176 | tf_op jit(solution)/shard_map/ppermute | solution.py:33
  160.7 1.2 maximum_bitcast_fusion.7
  162.0 1.6 gather_fusion.7
  163.6 1.9 copy.80
  165.5 1.4 convolution_bitcast_fusion
  166.9 2.5 copy.81
  169.4 2.4 stack.153
  171.8 5.4 %fusion.2 = f32[4,16,16384]{2,1,0:T(8,128)} fusion(bf16[1,4,16,16384]{3,2,1,0:T(8,128)(2,1)} %param.9, f32[1,16,16384]{2,1,0:T(8,128)} %stack.156, f32[1,16,16384]{2,1,0:T(8,128)} %stack.155, f32[1,16,16384]{2,1,0:T(8,128)} %stack.154, f32[1,16,16384]{2,1,0:T(8,128)} %stack.153, f32[4,16]{1,0:T(4,128)S(1)} %shift-left_convert_fusion), kind=kLoop, calls=%fused_computation.12 | loop fusion | flops 7340032 | bytes 10486016 | tf_op jit(solution)/shard_map/jit(clip)/min | solution.py:65
  177.2 1.8 convolution_convert_fusion.2
  180.0 1.6 collective-permute-start.11
  182.1 2.6 stack.160
  184.7 1.2 stack.159
  185.9 1.2 stack.161
  187.4 1.2 stack.158
  188.6 5.9 %collective-permute-done.10 = bf16[1,16,2,1,16,256]{5,1,2,4,3,0:T(8,128)(2,1)} collective-permute-done((bf16[1,16,2,1,16,256]{5,1,2,4,3,0:T(8,128)(2,1)}, bf16[1,16,2,1,16,256]{5,1,2,4,3,0:T(8,128)(2,1)}, u32[]{:S(2)}, u32[]{:S(2)}) %collective-permute-start.10) | collective-permute-done | bytes 262176 | tf_op jit(solution)/shard_map/ppermute | solution.py:33
  194.5 1.2 maximum_bitcast_fusion.3
  196.7 1.2 copy.64
  198.1 1.4 fusion.10
  199.5 1.2 fusion.14
  202.3 2.0 subtract_convert_fusion
  204.3 60.0 %reduce-scatter.2.cloned.1.call-done = f32[4,16,2048]{2,1,0:T(8,128)} async-done(((f32[4,16,16384]{2,1,0:T(8,128)}), f32[4,16,2048]{2,1,0:T(8,128)}) %reduce-scatter.2.cloned.1.call-update) | async-done | bytes 524304 | tf_op jit(solution)/shard_map/reduce_scatter | solution.py:104
  264.2 1.9 divide_multiply_fusion
  (97 shorter events, 18.8 us)
Async XLA Ops:
  7.2 54.8 %all-gather.2.cloned.1.call-start = ((), (), s32[]{:S(2)}) async-start(), calls=%async_computation.1 | async-start | bytes 2359296 | tf_op jit(solution)/shard_map/all_gather | solution.py:73
  7.9 256.3 %reduce-scatter.2.cloned.1.call-start = ((), (), s32[]{:S(2)}) async-start(), calls=%async_computation.2 | async-start | bytes 4718592 | tf_op jit(solution)/shard_map/reduce_scatter | solution.py:104
  9.3 3.2 %collective-permute-start.12 = (bf16[1,16,2,1,16,256]{5,1,2,4,3,0:T(8,128)(2,1)S(1)}, bf16[1,16,2,1,16,256]{5,1,2,4,3,0:T(8,128)(2,1)S(1)}, u32[]{:S(2)}, u32[]{:S(2)}) collective-permute-start(bf16[1,16,2,1,16,256]{5,1,2,4,3,0:T(8,128)(2,1)S(1)} %get-tuple-element.21), channel_id=1, source_target_pairs={{0,1},{1,0},{2,3},{3,2},{4,5},{5,4},{6,7},{7,6},{8,9},{9,8},{10,11... | collective-permute-start | bytes 786440 | tf_op jit(solution)/shard_map/ppermute | solution.py:33
  9.8 9.3 %collective-permute-start.14 = (bf16[1,16,2,1,16,256]{5,1,3,2,4,0:T(8,128)(2,1)S(1)}, bf16[1,16,2,1,16,256]{5,1,3,2,4,0:T(8,128)(2,1)S(1)}, u32[]{:S(2)}, u32[]{:S(2)}) collective-permute-start(bf16[1,16,2,1,16,256]{5,1,3,2,4,0:T(8,128)(2,1)S(1)} %get-tuple-element.22), channel_id=1, source_target_pairs={{0,3},{1,2},{2,1},{3,0},{4,7},{5,6},{6,5},{7,4},{8,11},{9,10},{10,... | collective-permute-start | bytes 786440 | tf_op jit(solution)/shard_map/ppermute | solution.py:33
  12.4 12.5 %collective-permute-start.13 = (bf16[1,16,2,1,16,256]{5,1,2,4,3,0:T(8,128)(2,1)S(1)}, bf16[1,16,2,1,16,256]{5,1,2,4,3,0:T(8,128)(2,1)S(1)}, u32[]{:S(2)}, u32[]{:S(2)}) collective-permute-start(bf16[1,16,2,1,16,256]{5,1,2,4,3,0:T(8,128)(2,1)S(1)} %get-tuple-element.23), channel_id=1, source_target_pairs={{0,2},{1,3},{2,0},{3,1},{4,6},{5,7},{6,4},{7,5},{8,10},{9,11},{10,... | collective-permute-start | bytes 786440 | tf_op jit(solution)/shard_map/ppermute | solution.py:33
  63.6 1.6 copy-start
  63.7 4.3 %copy-start.7 = (bf16[2,8,128,128]{3,2,1,0:T(8,128)(2,1)}, bf16[2,8,128,128]{3,2,1,0:T(8,128)(2,1)S(1)}, u32[]{:S(2)}) copy-start(bf16[2,8,128,128]{3,2,1,0:T(8,128)(2,1)S(1)} %copy.114) | copy-start | bytes 1572868
  63.9 2.0 copy-start.5
  65.9 5.4 %collective-permute-start = (bf16[1,16,2,1,16,256]{5,1,2,4,3,0:T(8,128)(2,1)S(1)}, bf16[1,16,2,1,16,256]{5,1,2,4,3,0:T(8,128)(2,1)S(1)}, u32[]{:S(2)}, u32[]{:S(2)}) collective-permute-start(bf16[1,16,2,1,16,256]{5,1,2,4,3,0:T(8,128)(2,1)S(1)} %get-tuple-element.37), channel_id=1, source_target_pairs={{0,1},{1,0},{2,3},{3,2},{4,5},{5,4},{6,7},{7,6},{8,9},{9,8},{10,11... | collective-permute-start | bytes 786440 | tf_op jit(solution)/shard_map/ppermute | solution.py:33
  65.9 8.3 %collective-permute-start.2 = (bf16[1,16,2,1,16,256]{5,1,3,2,4,0:T(8,128)(2,1)S(1)}, bf16[1,16,2,1,16,256]{5,1,3,2,4,0:T(8,128)(2,1)S(1)}, u32[]{:S(2)}, u32[]{:S(2)}) collective-permute-start(bf16[1,16,2,1,16,256]{5,1,3,2,4,0:T(8,128)(2,1)S(1)} %get-tuple-element.38), channel_id=1, source_target_pairs={{0,3},{1,2},{2,1},{3,0},{4,7},{5,6},{6,5},{7,4},{8,11},{9,10},{10,... | collective-permute-start | bytes 786440 | tf_op jit(solution)/shard_map/ppermute | solution.py:33
  67.5 13.3 %collective-permute-start.1 = (bf16[1,16,2,1,16,256]{5,1,2,4,3,0:T(8,128)(2,1)S(1)}, bf16[1,16,2,1,16,256]{5,1,2,4,3,0:T(8,128)(2,1)S(1)}, u32[]{:S(2)}, u32[]{:S(2)}) collective-permute-start(bf16[1,16,2,1,16,256]{5,1,2,4,3,0:T(8,128)(2,1)S(1)} %get-tuple-element.39), channel_id=1, source_target_pairs={{0,2},{1,3},{2,0},{3,1},{4,6},{5,7},{6,4},{7,5},{8,10},{9,11},{10,... | collective-permute-start | bytes 786440 | tf_op jit(solution)/shard_map/ppermute | solution.py:33
  68.6 15.8 %copy-start.8 = (bf16[2,8,128,128]{3,2,1,0:T(8,128)(2,1)}, bf16[2,8,128,128]{3,2,1,0:T(8,128)(2,1)S(1)}, u32[]{:S(2)}) copy-start(bf16[2,8,128,128]{3,2,1,0:T(8,128)(2,1)S(1)} %copy.112) | copy-start | bytes 1572868
  69.6 17.9 %collective-permute-start.15 = (bf16[1,16,2,1,16,256]{5,1,2,4,3,0:T(8,128)(2,1)}, bf16[1,16,2,1,16,256]{5,1,2,4,3,0:T(8,128)(2,1)}, u32[]{:S(2)}, u32[]{:S(2)}) collective-permute-start(bf16[1,16,2,1,16,256]{5,1,2,4,3,0:T(8,128)(2,1)} %get-tuple-element.17), channel_id=1, source_target_pairs={{0,1},{1,0},{2,3},{3,2},{4,5},{5,4},{6,7},{7,6},{8,9},{9,8},{10,11... | collective-permute-start | bytes 786440 | tf_op jit(solution)/shard_map/ppermute | solution.py:33
  69.6 19.3 %collective-permute-start.17 = (bf16[1,16,2,1,16,256]{5,1,3,2,4,0:T(8,128)(2,1)}, bf16[1,16,2,1,16,256]{5,1,3,2,4,0:T(8,128)(2,1)}, u32[]{:S(2)}, u32[]{:S(2)}) collective-permute-start(bf16[1,16,2,1,16,256]{5,1,3,2,4,0:T(8,128)(2,1)} %get-tuple-element.18), channel_id=1, source_target_pairs={{0,3},{1,2},{2,1},{3,0},{4,7},{5,6},{6,5},{7,4},{8,11},{9,10},{10,... | collective-permute-start | bytes 786440 | tf_op jit(solution)/shard_map/ppermute | solution.py:33
  71.2 20.9 %collective-permute-start.16 = (bf16[1,16,2,1,16,256]{5,1,2,4,3,0:T(8,128)(2,1)}, bf16[1,16,2,1,16,256]{5,1,2,4,3,0:T(8,128)(2,1)}, u32[]{:S(2)}, u32[]{:S(2)}) collective-permute-start(bf16[1,16,2,1,16,256]{5,1,2,4,3,0:T(8,128)(2,1)} %get-tuple-element.19), channel_id=1, source_target_pairs={{0,2},{1,3},{2,0},{3,1},{4,6},{5,7},{6,4},{7,5},{8,10},{9,11},{10,... | collective-permute-start | bytes 786440 | tf_op jit(solution)/shard_map/ppermute | solution.py:33
  84.4 3.7 %copy-start.19 = (s32[4,16]{1,0:T(4,128)S(1)}, s32[4,16]{1,0:T(4,128)}, u32[]{:S(2)}) copy-start(s32[4,16]{1,0:T(4,128)} %param.8) | copy-start | bytes 772
  85.9 11.9 %collective-permute-start.3 = (bf16[1,16,2,1,16,256]{5,1,2,4,3,0:T(8,128)(2,1)}, bf16[1,16,2,1,16,256]{5,1,2,4,3,0:T(8,128)(2,1)}, u32[]{:S(2)}, u32[]{:S(2)}) collective-permute-start(bf16[1,16,2,1,16,256]{5,1,2,4,3,0:T(8,128)(2,1)} %get-tuple-element.33), channel_id=1, source_target_pairs={{0,1},{1,0},{2,3},{3,2},{4,5},{5,4},{6,7},{7,6},{8,9},{9,8},{10,11... | collective-permute-start | bytes 786440 | tf_op jit(solution)/shard_map/ppermute | solution.py:33
  85.9 11.9 %collective-permute-start.5 = (bf16[1,16,2,1,16,256]{5,1,3,2,4,0:T(8,128)(2,1)}, bf16[1,16,2,1,16,256]{5,1,3,2,4,0:T(8,128)(2,1)}, u32[]{:S(2)}, u32[]{:S(2)}) collective-permute-start(bf16[1,16,2,1,16,256]{5,1,3,2,4,0:T(8,128)(2,1)} %get-tuple-element.34), channel_id=1, source_target_pairs={{0,3},{1,2},{2,1},{3,0},{4,7},{5,6},{6,5},{7,4},{8,11},{9,10},{10,... | collective-permute-start | bytes 786440 | tf_op jit(solution)/shard_map/ppermute | solution.py:33
  87.5 15.3 %collective-permute-start.4 = (bf16[1,16,2,1,16,256]{5,1,2,4,3,0:T(8,128)(2,1)}, bf16[1,16,2,1,16,256]{5,1,2,4,3,0:T(8,128)(2,1)}, u32[]{:S(2)}, u32[]{:S(2)}) collective-permute-start(bf16[1,16,2,1,16,256]{5,1,2,4,3,0:T(8,128)(2,1)} %get-tuple-element.35), channel_id=1, source_target_pairs={{0,2},{1,3},{2,0},{3,1},{4,6},{5,7},{6,4},{7,5},{8,10},{9,11},{10,... | collective-permute-start | bytes 786440 | tf_op jit(solution)/shard_map/ppermute | solution.py:33
  93.4 9.4 %copy-start.17 = (bf16[1,1,16,2,1,16,256]{6,2,3,5,4,1,0:T(8,128)(2,1)S(1)}, bf16[1,1,16,2,1,16,256]{6,2,3,5,4,1,0:T(8,128)(2,1)}, u32[]{:S(2)}) copy-start(bf16[1,1,16,2,1,16,256]{6,2,3,5,4,1,0:T(8,128)(2,1)} %get-tuple-element.32) | copy-start | bytes 786436
  107.1 1.2 copy-start.18
  109.3 2.5 copy-start.16
  110.2 27.2 %collective-permute-start.6 = (bf16[1,16,2,1,16,256]{5,1,2,4,3,0:T(8,128)(2,1)}, bf16[1,16,2,1,16,256]{5,1,2,4,3,0:T(8,128)(2,1)}, u32[]{:S(2)}, u32[]{:S(2)}) collective-permute-start(bf16[1,16,2,1,16,256]{5,1,2,4,3,0:T(8,128)(2,1)} %get-tuple-element.29), channel_id=1, source_target_pairs={{0,1},{1,0},{2,3},{3,2},{4,5},{5,4},{6,7},{7,6},{8,9},{9,8},{10,11... | collective-permute-start | bytes 786440 | tf_op jit(solution)/shard_map/ppermute | solution.py:33
  110.2 27.2 %collective-permute-start.8 = (bf16[1,16,2,1,16,256]{5,1,3,2,4,0:T(8,128)(2,1)}, bf16[1,16,2,1,16,256]{5,1,3,2,4,0:T(8,128)(2,1)}, u32[]{:S(2)}, u32[]{:S(2)}) collective-permute-start(bf16[1,16,2,1,16,256]{5,1,3,2,4,0:T(8,128)(2,1)} %get-tuple-element.30), channel_id=1, source_target_pairs={{0,3},{1,2},{2,1},{3,0},{4,7},{5,6},{6,5},{7,4},{8,11},{9,10},{10,... | collective-permute-start | bytes 786440 | tf_op jit(solution)/shard_map/ppermute | solution.py:33
  114.4 4.3 %collective-permute-start.18 = (bf16[1,16,2,1,16,256]{5,1,2,4,3,0:T(8,128)(2,1)}, bf16[1,16,2,1,16,256]{5,1,2,4,3,0:T(8,128)(2,1)}, u32[]{:S(2)}, u32[]{:S(2)}) collective-permute-start(bf16[1,16,2,1,16,256]{5,1,2,4,3,0:T(8,128)(2,1)} %get-tuple-element.13), channel_id=1, source_target_pairs={{0,1},{1,0},{2,3},{3,2},{4,5},{5,4},{6,7},{7,6},{8,9},{9,8},{10,11... | collective-permute-start | bytes 786440 | tf_op jit(solution)/shard_map/ppermute | solution.py:33
  114.4 10.1 %collective-permute-start.20 = (bf16[1,16,2,1,16,256]{5,1,3,2,4,0:T(8,128)(2,1)}, bf16[1,16,2,1,16,256]{5,1,3,2,4,0:T(8,128)(2,1)}, u32[]{:S(2)}, u32[]{:S(2)}) collective-permute-start(bf16[1,16,2,1,16,256]{5,1,3,2,4,0:T(8,128)(2,1)} %get-tuple-element.14), channel_id=1, source_target_pairs={{0,3},{1,2},{2,1},{3,0},{4,7},{5,6},{6,5},{7,4},{8,11},{9,10},{10,... | collective-permute-start | bytes 786440 | tf_op jit(solution)/shard_map/ppermute | solution.py:33
  115.1 16.0 %collective-permute-start.19 = (bf16[1,16,2,1,16,256]{5,1,2,4,3,0:T(8,128)(2,1)}, bf16[1,16,2,1,16,256]{5,1,2,4,3,0:T(8,128)(2,1)}, u32[]{:S(2)}, u32[]{:S(2)}) collective-permute-start(bf16[1,16,2,1,16,256]{5,1,2,4,3,0:T(8,128)(2,1)} %get-tuple-element.15), channel_id=1, source_target_pairs={{0,2},{1,3},{2,0},{3,1},{4,6},{5,7},{6,4},{7,5},{8,10},{9,11},{10,... | collective-permute-start | bytes 786440 | tf_op jit(solution)/shard_map/ppermute | solution.py:33
  117.3 13.8 %copy-start.15 = (f32[16,128,128]{2,1,0:T(8,128)}, f32[16,128,128]{2,1,0:T(8,128)S(1)}, u32[]{:S(2)}) copy-start(f32[16,128,128]{2,1,0:T(8,128)S(1)} %fusion.16) | copy-start | bytes 3145732
  118.7 18.8 %collective-permute-start.7 = (bf16[1,16,2,1,16,256]{5,1,2,4,3,0:T(8,128)(2,1)}, bf16[1,16,2,1,16,256]{5,1,2,4,3,0:T(8,128)(2,1)}, u32[]{:S(2)}, u32[]{:S(2)}) collective-permute-start(bf16[1,16,2,1,16,256]{5,1,2,4,3,0:T(8,128)(2,1)} %get-tuple-element.31), channel_id=1, source_target_pairs={{0,2},{1,3},{2,0},{3,1},{4,6},{5,7},{6,4},{7,5},{8,10},{9,11},{10,... | collective-permute-start | bytes 786440 | tf_op jit(solution)/shard_map/ppermute | solution.py:33
  136.0 1.0 copy-start.9
  146.2 6.2 %collective-permute-start.21 = (bf16[1,16,2,1,16,256]{5,1,2,4,3,0:T(8,128)(2,1)}, bf16[1,16,2,1,16,256]{5,1,2,4,3,0:T(8,128)(2,1)}, u32[]{:S(2)}, u32[]{:S(2)}) collective-permute-start(bf16[1,16,2,1,16,256]{5,1,2,4,3,0:T(8,128)(2,1)} %get-tuple-element.9), channel_id=1, source_target_pairs={{0,1},{1,0},{2,3},{3,2},{4,5},{5,4},{6,7},{7,6},{8,9},{9,8},{10,11... | collective-permute-start | bytes 786440 | tf_op jit(solution)/shard_map/ppermute | solution.py:33
  146.2 8.6 %collective-permute-start.23 = (bf16[1,16,2,1,16,256]{5,1,3,2,4,0:T(8,128)(2,1)}, bf16[1,16,2,1,16,256]{5,1,3,2,4,0:T(8,128)(2,1)}, u32[]{:S(2)}, u32[]{:S(2)}) collective-permute-start(bf16[1,16,2,1,16,256]{5,1,3,2,4,0:T(8,128)(2,1)} %get-tuple-element.10), channel_id=1, source_target_pairs={{0,3},{1,2},{2,1},{3,0},{4,7},{5,6},{6,5},{7,4},{8,11},{9,10},{10,... | collective-permute-start | bytes 786440 | tf_op jit(solution)/shard_map/ppermute | solution.py:33
  147.8 13.0 %collective-permute-start.22 = (bf16[1,16,2,1,16,256]{5,1,2,4,3,0:T(8,128)(2,1)}, bf16[1,16,2,1,16,256]{5,1,2,4,3,0:T(8,128)(2,1)}, u32[]{:S(2)}, u32[]{:S(2)}) collective-permute-start(bf16[1,16,2,1,16,256]{5,1,2,4,3,0:T(8,128)(2,1)} %get-tuple-element.11), channel_id=1, source_target_pairs={{0,2},{1,3},{2,0},{3,1},{4,6},{5,7},{6,4},{7,5},{8,10},{9,11},{10,... | collective-permute-start | bytes 786440 | tf_op jit(solution)/shard_map/ppermute | solution.py:33
  163.6 1.9 copy-start.1
  180.0 8.6 %collective-permute-start.9 = (bf16[1,16,2,1,16,256]{5,1,2,4,3,0:T(8,128)(2,1)}, bf16[1,16,2,1,16,256]{5,1,2,4,3,0:T(8,128)(2,1)}, u32[]{:S(2)}, u32[]{:S(2)}) collective-permute-start(bf16[1,16,2,1,16,256]{5,1,2,4,3,0:T(8,128)(2,1)} %get-tuple-element.25), channel_id=1, source_target_pairs={{0,1},{1,0},{2,3},{3,2},{4,5},{5,4},{6,7},{7,6},{8,9},{9,8},{10,11... | collective-permute-start | bytes 786440 | tf_op jit(solution)/shard_map/ppermute | solution.py:33
  180.0 8.6 %collective-permute-start.11 = (bf16[1,16,2,1,16,256]{5,1,3,2,4,0:T(8,128)(2,1)}, bf16[1,16,2,1,16,256]{5,1,3,2,4,0:T(8,128)(2,1)}, u32[]{:S(2)}, u32[]{:S(2)}) collective-permute-start(bf16[1,16,2,1,16,256]{5,1,3,2,4,0:T(8,128)(2,1)} %get-tuple-element.26), channel_id=1, source_target_pairs={{0,3},{1,2},{2,1},{3,0},{4,7},{5,6},{6,5},{7,4},{8,11},{9,10},{10,... | collective-permute-start | bytes 786440 | tf_op jit(solution)/shard_map/ppermute | solution.py:33
  181.6 13.0 %collective-permute-start.10 = (bf16[1,16,2,1,16,256]{5,1,2,4,3,0:T(8,128)(2,1)}, bf16[1,16,2,1,16,256]{5,1,2,4,3,0:T(8,128)(2,1)}, u32[]{:S(2)}, u32[]{:S(2)}) collective-permute-start(bf16[1,16,2,1,16,256]{5,1,2,4,3,0:T(8,128)(2,1)} %get-tuple-element.27), channel_id=1, source_target_pairs={{0,2},{1,3},{2,0},{3,1},{4,6},{5,7},{6,4},{7,5},{8,10},{9,11},{10,... | collective-permute-start | bytes 786440 | tf_op jit(solution)/shard_map/ppermute | solution.py:33
  185.9 1.5 copy-start.3
  196.7 1.3 copy-start.6
  196.7 1.4 copy-start.10
  197.9 1.6 copy-start.2
  198.1 2.7 copy-start.13
  198.1 2.7 copy-start.14
  199.5 2.1 copy-start.4
  199.5 2.4 copy-start.11
  199.5 2.8 %copy-start.12 = (f32[1,1,16,16384]{3,2,1,0:T(8,128)S(1)}, f32[1,1,16,16384]{3,2,1,0:T(8,128)}, u32[]{:S(2)}) copy-start(f32[1,1,16,16384]{3,2,1,0:T(8,128)} %stack.159) | copy-start | bytes 3145732
Sparse Core Ops, SparseCore 0:
  10.2 51.7 all-gather.1
  177.3 86.8 reduce-scatter.1
